TPU v7x, 32 devices: a whole 2x2x4 slice. The times are simulated.
32 devices in a mesh: wide: 8 (over z, x), ffn: 4 (over y, core).
Axes of the slice: x: 2, y: 2, z: 4, core: 2. Of those that a mesh axis runs over, the one named last changes fastest.
Arguments:
- hidden_in: bfloat16 [8192, 1024], P(('wide', 'ffn')), may hold values from -6 to 6
- doc_ids: int32 [8192], P(('wide', 'ffn')), may hold values from -1 to 3, as said below
- out_grad: bfloat16 [8192, 1024], P(('wide', 'ffn')), may hold values from -6 to 6
- w_query: bfloat16 [1024, 1024], P(('wide', 'ffn')), may hold values from -0.25 to 0.25
- b_query: bfloat16 [1024], P(('wide', 'ffn')), may hold values from -1.1953125 to 1.1953125
- w_key: bfloat16 [1024, 1024], P(('wide', 'ffn')), may hold values from -0.25 to 0.25
- w_value: bfloat16 [1024, 1024], P(('wide', 'ffn')), may hold values from -0.1875 to 0.1875
- b_value: bfloat16 [1024], P(('wide', 'ffn')), may hold values from -1.1953125 to 1.1953125
- w_output: bfloat16 [1024, 1024], P(('wide', 'ffn')), may hold values from -0.75 to 0.75
- b_output: bfloat16 [1024], P(('wide', 'ffn')), may hold values from -1.1953125 to 1.1953125
- attn_gain: bfloat16 [1024], P(('wide', 'ffn')), may hold values from 0.25 to 1.75
- attn_shift: bfloat16 [1024], P(('wide', 'ffn')), may hold values from -1.1953125 to 1.1953125
- w_up: bfloat16 [1024, 4096], P('wide', 'ffn'), may hold values from -0.1875 to 0.1875
- b_up: bfloat16 [4096], P(('wide', 'ffn')), may hold values from -1.1953125 to 1.1953125
- w_down: bfloat16 [4096, 1024], P('ffn', 'wide'), may hold values from -0.09375 to 0.09375
- b_down: bfloat16 [1024], P(('wide', 'ffn')), may hold values from -1.1953125 to 1.1953125
- ffn_gain: bfloat16 [1024], P(('wide', 'ffn')), may hold values from 0.25 to 1.75
- ffn_shift: bfloat16 [1024], P(('wide', 'ffn')), may hold values from -1.1953125 to 1.1953125
Outputs:
- out_rows: bfloat16 [8192, 1024], P(('wide', 'ffn'))
- grad_input: float32 [8192, 1024], P(('wide', 'ffn'))
- grad_w_query: float32 [1024, 1024], P(('wide', 'ffn'))
- grad_b_query: float32 [1024], P(('wide', 'ffn'))
- grad_w_key: float32 [1024, 1024], P(('wide', 'ffn'))
- grad_w_value: float32 [1024, 1024], P(('wide', 'ffn'))
- grad_b_value: float32 [1024], P(('wide', 'ffn'))
- grad_w_output: float32 [1024, 1024], P(('wide', 'ffn'))
- grad_b_output: float32 [1024], P(('wide', 'ffn'))
- grad_attn_gain: float32 [1024], P(('wide', 'ffn'))
- grad_attn_shift: float32 [1024], P(('wide', 'ffn'))
- grad_w_up: float32 [1024, 4096], P('wide', 'ffn')
- grad_b_up: float32 [4096], P(('wide', 'ffn'))
- grad_w_down: float32 [4096, 1024], P('ffn', 'wide')
- grad_b_down: float32 [1024], P(('wide', 'ffn'))
- grad_ffn_gain: float32 [1024], P(('wide', 'ffn'))
- grad_ffn_shift: float32 [1024], P(('wide', 'ffn'))
Inputs may be any that keep to these rules, and one draw needn't show every extreme that they name: `doc_ids`: within each device's 256 rows either all rows are item 0 (one item of 256 residues), or items 0 to c - 1 of 64 residues each fill the first c * 64 rows for some c of 1 to 4 and the remaining rows are -1. In every draw some device holds one full item and some device holds four short ones.
All inputs are finite; a program needn't handle non-finite values.
Results may differ from a plain program's by a relative error of at most 0.015.
The roundings to bfloat16 on the way count: a program that leaves them out, or rounds other values in their place, can miss the bound.
Values may be sent and summed in bfloat16 or wider, within the bound.
No kernel may reach another device: no remote copies, remote signals or barrier semaphores. Data moves between devices by JAX's collectives and lax.ppermute only.
A program may use at most 128 MiB of HBM per device.

v0:
```python
import math
import jax
import jax.numpy as jnp
from jax import lax
from jax.sharding import PartitionSpec as P

D = 1024
HEADS = 16
HEAD_DIM = 64
norm_eps = 1e-12


def matmul(left, right):
    return jnp.dot(left, right, preferred_element_type=jnp.float32)


def matmul_tn(left, right):
    return lax.dot_general(
        left, right, (((0,), (0,)), ((), ())), preferred_element_type=jnp.float32
    )


def matmul_nt(left, right):
    return lax.dot_general(
        left, right, (((1,), (1,)), ((), ())), preferred_element_type=jnp.float32
    )


def layer_norm(values, gain, shift):
    centre = values - jnp.mean(values, axis=-1, keepdims=True)
    inverse = lax.rsqrt(jnp.mean(centre * centre, axis=-1, keepdims=True) + norm_eps)
    normed = centre * inverse
    return (normed * gain + shift, normed, inverse)


def norm_back(grad, normed, inverse):
    return inverse * (
        grad
        - jnp.mean(grad, axis=-1, keepdims=True)
        - normed * jnp.mean(grad * normed, axis=-1, keepdims=True)
    )


def gelu_exact(values):
    return 0.5 * values * (1.0 + jax.scipy.special.erf(values * (1.0 / math.sqrt(2.0))))


def gelu_slope(values):
    return 0.5 * (1.0 + jax.scipy.special.erf(values * (1.0 / math.sqrt(2.0)))) + values * jnp.exp(
        -0.5 * values * values
    ) * (1.0 / math.sqrt(2.0 * math.pi))


def masked_scores(queries, key_rows, allowed, score_scale):
    scores = (
        jnp.einsum("qhd,khd->hqk", queries, key_rows, preferred_element_type=jnp.float32)
        * score_scale
    )
    return jnp.where(allowed[None, :, :], scores, -1000000000.0)


def column_sum(values):
    return jnp.sum(values.astype(jnp.float32), axis=0)


def body(
    hidden_in,
    doc_ids,
    out_grad,
    w_query,
    b_query,
    w_key,
    w_value,
    b_value,
    w_output,
    b_output,
    attn_gain,
    attn_shift,
    w_up,
    b_up,
    w_down,
    b_down,
    ffn_gain,
    ffn_shift,
):
    gathered = (
        lax.all_gather(w_query, ("wide", "ffn"), axis=0, tiled=True),
        lax.all_gather(w_key, ("wide", "ffn"), axis=0, tiled=True),
        lax.all_gather(w_value, ("wide", "ffn"), axis=0, tiled=True),
        lax.all_gather(w_output, ("wide", "ffn"), axis=0, tiled=True),
        lax.all_gather(b_query, ("wide", "ffn"), axis=0, tiled=True),
        lax.all_gather(b_value, ("wide", "ffn"), axis=0, tiled=True),
        lax.all_gather(b_output, ("wide", "ffn"), axis=0, tiled=True),
        lax.all_gather(attn_gain, ("wide", "ffn"), axis=0, tiled=True),
        lax.all_gather(attn_shift, ("wide", "ffn"), axis=0, tiled=True),
        lax.all_gather(b_up, ("wide", "ffn"), axis=0, tiled=True),
        lax.all_gather(b_down, ("wide", "ffn"), axis=0, tiled=True),
        lax.all_gather(ffn_gain, ("wide", "ffn"), axis=0, tiled=True),
        lax.all_gather(ffn_shift, ("wide", "ffn"), axis=0, tiled=True),
    )
    query_full, key_full, value_full, output_full = (
        gathered[0],
        gathered[1],
        gathered[2],
        gathered[3],
    )
    (
        bias_query,
        bias_value,
        bias_output,
        gain_one,
        shift_one,
        bias_up_all,
        bias_down,
        gain_two,
        shift_two,
    ) = [vector.astype(jnp.float32) for vector in gathered[4:]]
    up_part, down_part = (
        lax.all_gather(w_up, "wide", axis=0, tiled=True),
        lax.all_gather(w_down, "wide", axis=1, tiled=True),
    )
    row_count = hidden_in.shape[0]
    score_scale = HEAD_DIM ** (-0.5)
    residual_in = hidden_in.astype(jnp.float32)
    queries = (
        (matmul(hidden_in, query_full) + bias_query)
        .astype(jnp.bfloat16)
        .reshape(row_count, HEADS, HEAD_DIM)
    )
    key_rows = matmul(hidden_in, key_full).astype(jnp.bfloat16).reshape(row_count, HEADS, HEAD_DIM)
    value_rows = (
        (matmul(hidden_in, value_full) + bias_value)
        .astype(jnp.bfloat16)
        .reshape(row_count, HEADS, HEAD_DIM)
    )
    allowed = doc_ids[:, None] == doc_ids[None, :]
    scores = masked_scores(queries, key_rows, allowed, score_scale)
    top_score = jnp.max(scores, axis=-1, keepdims=True)
    expo_terms = jnp.exp(scores - top_score)
    total_sum = jnp.sum(expo_terms, axis=-1, keepdims=True)
    attn_probs = expo_terms / total_sum
    log_total = top_score + jnp.log(total_sum)
    context = (
        jnp.einsum(
            "hqk,khd->qhd",
            attn_probs.astype(jnp.bfloat16),
            value_rows,
            preferred_element_type=jnp.float32,
        )
        .reshape(row_count, D)
        .astype(jnp.bfloat16)
    )
    attended = matmul(context, output_full) + bias_output
    normed_out, normed_one, inverse_one = layer_norm(residual_in + attended, gain_one, shift_one)
    normed_low = normed_out.astype(jnp.bfloat16)
    slice_len = up_part.shape[1]
    member = lax.axis_index("ffn")
    bias_up = lax.dynamic_slice_in_dim(bias_up_all, member * slice_len, slice_len)
    group_rows = lax.all_gather(normed_low, "ffn", axis=0, tiled=True)
    up_rows = matmul(group_rows, up_part) + bias_up
    active_low = gelu_exact(up_rows).astype(jnp.bfloat16)
    down_rows = (
        lax.psum_scatter(
            matmul(active_low, down_part).astype(jnp.bfloat16),
            "ffn",
            scatter_dimension=0,
            tiled=True,
        ).astype(jnp.float32)
        + bias_down
    )
    layer_out, normed_two, inverse_two = layer_norm(normed_out + down_rows, gain_two, shift_two)
    grad_out = out_grad.astype(jnp.float32)
    grad_gain_two = jnp.sum(grad_out * normed_two, axis=0)
    grad_shift_two = jnp.sum(grad_out, axis=0)
    grad_two = norm_back(grad_out * gain_two, normed_two, inverse_two)
    grad_two_low = grad_two.astype(jnp.bfloat16)
    grad_bias_down = column_sum(grad_two_low)
    grad_group = lax.all_gather(grad_two_low, "ffn", axis=0, tiled=True)
    grad_active = matmul_nt(grad_group, down_part)
    grad_up_low = (grad_active * gelu_slope(up_rows)).astype(jnp.bfloat16)
    grad_bias_up = lax.dynamic_update_slice_in_dim(
        jnp.zeros(bias_up_all.shape, jnp.float32), column_sum(grad_up_low), member * slice_len, 0
    )
    grad_up_w = matmul_tn(group_rows, grad_up_low)
    grad_down_w = matmul_tn(active_low, grad_group)
    grad_one = grad_two + lax.psum_scatter(
        matmul_nt(grad_up_low, up_part).astype(jnp.bfloat16), "ffn", scatter_dimension=0, tiled=True
    ).astype(jnp.float32)
    grad_up_w, grad_down_w = (
        lax.psum_scatter(grad_up_w, "wide", scatter_dimension=0, tiled=True),
        lax.psum_scatter(grad_down_w, "wide", scatter_dimension=1, tiled=True),
    )
    grad_gain_one = jnp.sum(grad_one * normed_one, axis=0)
    grad_shift_one = jnp.sum(grad_one, axis=0)
    grad_z_one = norm_back(grad_one * gain_one, normed_one, inverse_one)
    grad_att_low = grad_z_one.astype(jnp.bfloat16)
    grad_bias_output = column_sum(grad_att_low)
    grad_output_w = matmul_tn(context, grad_att_low)
    grad_context = (
        matmul_nt(grad_att_low, output_full)
        .astype(jnp.bfloat16)
        .reshape(row_count, HEADS, HEAD_DIM)
    )
    scores = masked_scores(queries, key_rows, allowed, score_scale)
    attn_probs = jnp.exp(scores - log_total)
    grad_probs = jnp.einsum(
        "qhd,khd->hqk", grad_context, value_rows, preferred_element_type=jnp.float32
    )
    grad_values = (
        jnp.einsum(
            "hqk,qhd->khd",
            attn_probs.astype(jnp.bfloat16),
            grad_context,
            preferred_element_type=jnp.float32,
        )
        .astype(jnp.bfloat16)
        .reshape(row_count, D)
    )
    row_inner = jnp.sum(attn_probs * grad_probs, axis=-1, keepdims=True)
    grad_scores = (attn_probs * (grad_probs - row_inner)).astype(jnp.bfloat16)
    grad_queries = (
        (
            jnp.einsum("hqk,khd->qhd", grad_scores, key_rows, preferred_element_type=jnp.float32)
            * score_scale
        )
        .astype(jnp.bfloat16)
        .reshape(row_count, D)
    )
    grad_keys = (
        (
            jnp.einsum("hqk,qhd->khd", grad_scores, queries, preferred_element_type=jnp.float32)
            * score_scale
        )
        .astype(jnp.bfloat16)
        .reshape(row_count, D)
    )
    grad_query_w = matmul_tn(hidden_in, grad_queries)
    grad_key_w = matmul_tn(hidden_in, grad_keys)
    grad_value_w = matmul_tn(hidden_in, grad_values)
    grad_input = (
        grad_z_one
        + matmul_nt(grad_queries, query_full)
        + matmul_nt(grad_keys, key_full)
        + matmul_nt(grad_values, value_full)
    )
    summed = (
        lax.psum_scatter(grad_query_w, ("wide", "ffn"), scatter_dimension=0, tiled=True),
        lax.psum_scatter(grad_key_w, ("wide", "ffn"), scatter_dimension=0, tiled=True),
        lax.psum_scatter(grad_value_w, ("wide", "ffn"), scatter_dimension=0, tiled=True),
        lax.psum_scatter(grad_output_w, ("wide", "ffn"), scatter_dimension=0, tiled=True),
        lax.psum_scatter(
            column_sum(grad_queries), ("wide", "ffn"), scatter_dimension=0, tiled=True
        ),
        lax.psum_scatter(column_sum(grad_values), ("wide", "ffn"), scatter_dimension=0, tiled=True),
        lax.psum_scatter(grad_bias_output, ("wide", "ffn"), scatter_dimension=0, tiled=True),
        lax.psum_scatter(grad_gain_one, ("wide", "ffn"), scatter_dimension=0, tiled=True),
        lax.psum_scatter(grad_shift_one, ("wide", "ffn"), scatter_dimension=0, tiled=True),
        lax.psum_scatter(grad_bias_up, ("wide", "ffn"), scatter_dimension=0, tiled=True),
        lax.psum_scatter(grad_bias_down, ("wide", "ffn"), scatter_dimension=0, tiled=True),
        lax.psum_scatter(grad_gain_two, ("wide", "ffn"), scatter_dimension=0, tiled=True),
        lax.psum_scatter(grad_shift_two, ("wide", "ffn"), scatter_dimension=0, tiled=True),
    )
    return (
        layer_out.astype(jnp.bfloat16),
        grad_input,
        summed[0],
        summed[4],
        summed[1],
        summed[2],
        summed[5],
        summed[3],
        summed[6],
        summed[7],
        summed[8],
        grad_up_w,
        summed[9],
        grad_down_w,
        summed[10],
        summed[11],
        summed[12],
    )


def solution(mesh):
    in_specs = (
        P(("wide", "ffn"), None),
        P(("wide", "ffn")),
        P(("wide", "ffn"), None),
        P(("wide", "ffn"), None),
        P(("wide", "ffn")),
        P(("wide", "ffn"), None),
        P(("wide", "ffn"), None),
        P(("wide", "ffn")),
        P(("wide", "ffn"), None),
        P(("wide", "ffn")),
        P(("wide", "ffn")),
        P(("wide", "ffn")),
        P("wide", "ffn"),
        P(("wide", "ffn")),
        P("ffn", "wide"),
        P(("wide", "ffn")),
        P(("wide", "ffn")),
        P(("wide", "ffn")),
    )
    out_specs = (
        P(("wide", "ffn"), None),
        P(("wide", "ffn"), None),
        P(("wide", "ffn"), None),
        P(("wide", "ffn")),
        P(("wide", "ffn"), None),
        P(("wide", "ffn"), None),
        P(("wide", "ffn")),
        P(("wide", "ffn"), None),
        P(("wide", "ffn")),
        P(("wide", "ffn")),
        P(("wide", "ffn")),
        P("wide", "ffn"),
        P(("wide", "ffn")),
        P("ffn", "wide"),
        P(("wide", "ffn")),
        P(("wide", "ffn")),
        P(("wide", "ffn")),
    )
    return jax.shard_map(body, mesh=mesh, in_specs=in_specs, out_specs=out_specs, check_vma=False)
```

profile of v0, /device:TPU:0, one launch (start us, length us, event | category | flops | bytes accessed | tf_op | source)
XLA Modules:
  0.0 1234.9 jit_solution(16796781667847248619)
XLA Ops:
  17.3 42.2 %all-reduce.18 = (bf16[1024]{0:T(1024)(128)(2,1)S(1)}, bf16[1024]{0:T(1024)(128)(2,1)S(1)}, bf16[1024]{0:T(1024)(128)(2,1)S(1)}, bf16[1024]{0:T(1024)(128)(2,1)S...) all-reduce(bf16[1024]{0:T(1024)(128)(2,1)S(1)} %dynamic-update-slic, ...), channel_id=1, replica_groups=mesh['wide'=8,'ffn'=4] {'wide','ffn'}, use_global_device_ids=true, to_apply=%add | all-reduce | flops 8192 | bytes 32768
  60.5 9.6 all-gather.12.cloned.1.call-done
  72.7 55.4 %all-gather.14.cloned.1.call-done = bf16[1024,1024]{1,0:T(8,128)(2,1)} async-done(((bf16[32,1024]{1,0:T(8,128)(2,1)}), bf16[1024,1024]{1,0:T(8,128)(2,1)}) %all-gather.14.cloned.1.call-update) | async-done | bytes 2097168 | tf_op jit(solution)/shard_map/all_gather | solution.py:88
  130.6 55.5 %all-gather.10.cloned.1.call-done = bf16[1024,1024]{1,0:T(8,128)(2,1)} async-done(((bf16[32,1024]{1,0:T(8,128)(2,1)}), bf16[1024,1024]{1,0:T(8,128)(2,1)}) %all-gather.10.cloned.1.call-update) | async-done | bytes 2097168 | tf_op jit(solution)/shard_map/all_gather | solution.py:89
  192.3 51.6 %all-gather.16.cloned.1.call-done = bf16[1024,1024]{1,0:T(8,128)(2,1)} async-done(((bf16[32,1024]{1,0:T(8,128)(2,1)}), bf16[1024,1024]{1,0:T(8,128)(2,1)}) %all-gather.16.cloned.1.call-update) | async-done | bytes 2097168 | tf_op jit(solution)/shard_map/all_gather | solution.py:90
  248.5 39.9 %all-gather = bf16[32,1,128]{2,1,0:T(2,128)(2,1)S(1)} all-gather(bf16[1,1,128]{2,1,0:T(2,128)(2,1)S(1)} %bitcast.90), channel_id=1, replica_groups=mesh['wide'=8,'ffn'=4] {'wide','ffn'}, dimensions={0}, use_global_device_ids=true | all-gather | bytes 8448 | tf_op jit(solution)/shard_map/all_gather | solution.py:96
  288.4 5.6 all-gather.20.cloned.1.call-done
  294.0 23.2 %all-gather.18.cloned.1.call-done = bf16[1024,1024]{1,0:T(8,128)(2,1)} async-done(((bf16[256,1024]{1,0:T(8,128)(2,1)}), bf16[1024,1024]{1,0:T(8,128)(2,1)}) %all-gather.18.cloned.1.call-update) | async-done | bytes 2097168 | tf_op jit(solution)/shard_map/all_gather | solution.py:159
  317.2 7.4 multiply_convert_fusion.1
  324.6 45.0 %all-gather.22.cloned.1.call-done = bf16[1024,1024]{1,0:T(8,128)(2,1)} async-done(((bf16[1024,128]{1,0:T(8,128)(2,1)}), bf16[1024,1024]{1,0:T(8,128)(2,1)}) %all-gather.22.cloned.1.call-update) | async-done | bytes 2097168 | tf_op jit(solution)/shard_map/all_gather | solution.py:120
  369.6 5.9 convolution_convert_fusion.1
  375.6 29.4 %reduce-scatter.15.cloned.1.call-done = bf16[256,1024]{1,0:T(8,128)(2,1)} async-done(((bf16[1024,1024]{1,0:T(8,128)(2,1)}), bf16[256,1024]{1,0:T(8,128)(2,1)}) %reduce-scatter.15.cloned.1.call-update) | async-done | bytes 524304 | tf_op jit(solution)/shard_map/reduce_scatter | solution.py:163
  408.9 22.7 %all-gather.24.cloned.1.call-done = bf16[1024,1024]{1,0:T(8,128)(2,1)} async-done(((bf16[256,1024]{1,0:T(8,128)(2,1)}), bf16[1024,1024]{1,0:T(8,128)(2,1)}) %all-gather.24.cloned.1.call-update) | async-done | bytes 2097168 | tf_op jit(solution)/shard_map/all_gather | solution.py:178
  431.5 6.6 convert_reduce_fusion
  443.3 6.6 fusion.38
  450.1 7.0 fusion.37
  457.2 17.3 %reduce-scatter.17.cloned.1.call-done = bf16[256,1024]{1,0:T(8,128)(2,1)} async-done(((bf16[1024,1024]{1,0:T(8,128)(2,1)}), bf16[256,1024]{1,0:T(8,128)(2,1)}) %reduce-scatter.17.cloned.1.call-update) | async-done | bytes 524304 | tf_op jit(solution)/shard_map/reduce_scatter | solution.py:186
  485.4 5.5 copy.80
  521.0 41.5 %all-reduce.17 = (f32[1024]{0:T(1024)S(1)}, f32[1024]{0:T(1024)S(1)}, f32[1024]{0:T(1024)S(1)}, f32[1024]{0:T(1024)S(1)}, f32[1024]{0:T(1024)S(1)}, /*index=5*/f...) all-reduce(f32[1024]{0:T(1024)S(1)} %reduce_sum.186, ...), channel_id=5, replica_groups=mesh['wide'=8,'ffn'=4] {'wide','ffn'}, use_global_device_ids=true, to_apply=%region_15.16.clone | all-reduce | flops 12288 | bytes 98304
  573.8 85.9 %reduce-scatter.21.cloned.1.call-done = f32[128,1024]{1,0:T(8,128)} async-done(((f32[1024,1024]{1,0:T(8,128)}), f32[128,1024]{1,0:T(8,128)}) %reduce-scatter.21.cloned.1.call-update) | async-done | bytes 524304 | tf_op jit(solution)/shard_map/reduce_scatter | solution.py:190
  659.7 145.1 %reduce-scatter.29.cloned.1.call-done = f32[32,1024]{1,0:T(8,128)} async-done(((f32[1024,1024]{1,0:T(8,128)}), f32[32,1024]{1,0:T(8,128)}) %reduce-scatter.29.cloned.1.call-update) | async-done | bytes 131088
  804.8 141.1 %reduce-scatter.27.cloned.1.call-done = f32[32,1024]{1,0:T(8,128)} async-done(((f32[1024,1024]{1,0:T(8,128)}), f32[32,1024]{1,0:T(8,128)}) %reduce-scatter.27.cloned.1.call-update) | async-done | bytes 131088
  945.9 141.2 %reduce-scatter.25.cloned.1.call-done = f32[32,1024]{1,0:T(8,128)} async-done(((f32[1024,1024]{1,0:T(8,128)}), f32[32,1024]{1,0:T(8,128)}) %reduce-scatter.25.cloned.1.call-update) | async-done | bytes 131088
  1087.1 141.3 %reduce-scatter.19.cloned.1.call-done = f32[32,1024]{1,0:T(8,128)} async-done(((f32[1024,1024]{1,0:T(8,128)}), f32[32,1024]{1,0:T(8,128)}) %reduce-scatter.19.cloned.1.call-update) | async-done | bytes 131088 | tf_op jit(solution)/shard_map/reduce_scatter | solution.py:250
  (170 shorter events, 88.1 us)
Async XLA Ops:
  7.2 62.8 %all-gather.12.cloned.1.call-start = ((), (), s32[]{:S(2)}) async-start(), calls=%async_computation.9 | async-start | bytes 2162688 | tf_op jit(solution)/shard_map/all_gather | solution.py:87
  7.9 120.2 %all-gather.14.cloned.1.call-start = ((), (), s32[]{:S(2)}) async-start(), calls=%async_computation.10 | async-start | bytes 2162688 | tf_op jit(solution)/shard_map/all_gather | solution.py:88
  8.7 177.4 %all-gather.10.cloned.1.call-start = ((), (), s32[]{:S(2)}) async-start(), calls=%async_computation.8 | async-start | bytes 2162688 | tf_op jit(solution)/shard_map/all_gather | solution.py:89
  9.4 234.5 %all-gather.16.cloned.1.call-start = ((), (), s32[]{:S(2)}) async-start(), calls=%async_computation.11 | async-start | bytes 2162688 | tf_op jit(solution)/shard_map/all_gather | solution.py:90
  10.0 284.0 %all-gather.20.cloned.1.call-start = ((), (), s32[]{:S(2)}) async-start(), calls=%async_computation.13 | async-start | bytes 2359296 | tf_op jit(solution)/shard_map/all_gather | solution.py:119
  10.6 306.6 %all-gather.18.cloned.1.call-start = ((), (), s32[]{:S(2)}) async-start(), calls=%async_computation.12 | async-start | bytes 2621440 | tf_op jit(solution)/shard_map/all_gather | solution.py:159
  60.4 67.6 %copy-start.2 = (bf16[256,1024]{1,0:T(8,128)(2,1)S(1)}, bf16[256,1024]{1,0:T(8,128)(2,1)}, u32[]{:S(2)}) copy-start(bf16[256,1024]{1,0:T(8,128)(2,1)} %param.18) | copy-start | bytes 1572868
  72.7 115.9 %copy-start.14 = (bf16[256,1024]{0,1:T(8,128)(2,1)}, bf16[256,1024]{0,1:T(8,128)(2,1)S(1)}, u32[]{:S(2)}) copy-start(bf16[256,1024]{0,1:T(8,128)(2,1)S(1)} %copy.62) | copy-start | bytes 1572868
  130.6 58.0 %copy-start.13 = (bf16[256,1024]{0,1:T(8,128)(2,1)}, bf16[256,1024]{0,1:T(8,128)(2,1)S(1)}, u32[]{:S(2)}) copy-start(bf16[256,1024]{0,1:T(8,128)(2,1)S(1)} %copy.63) | copy-start | bytes 1572868
  192.3 54.0 %copy-start.22 = (bf16[16,64,256]{2,1,0:T(8,128)(2,1)}, bf16[16,64,256]{2,1,0:T(8,128)(2,1)S(1)}, u32[]{:S(2)}) copy-start(bf16[16,64,256]{2,1,0:T(8,128)(2,1)S(1)} %fusion.23) | copy-start | bytes 1572868
  247.7 121.9 %all-gather.22.cloned.1.call-start = ((), (), s32[]{:S(2)}) async-start(), calls=%async_computation.14 | async-start | bytes 2359296 | tf_op jit(solution)/shard_map/all_gather | solution.py:120
  248.5 156.6 %reduce-scatter.15.cloned.1.call-start = ((), (), s32[]{:S(2)}) async-start(), calls=%async_computation.15 | async-start | bytes 2621440 | tf_op jit(solution)/shard_map/reduce_scatter | solution.py:163
  375.5 31.3 %copy-start.16 = (bf16[256,1024]{1,0:T(8,128)(2,1)S(1)}, bf16[256,1024]{1,0:T(8,128)(2,1)}, u32[]{:S(2)}) copy-start(bf16[256,1024]{1,0:T(8,128)(2,1)} %param.20) | copy-start | bytes 1572868
  375.5 56.0 %all-gather.24.cloned.1.call-start = ((), (), s32[]{:S(2)}) async-start(), calls=%async_computation.16 | async-start | bytes 2621440 | tf_op jit(solution)/shard_map/all_gather | solution.py:178
  408.8 65.7 %reduce-scatter.17.cloned.1.call-start = ((), (), s32[]{:S(2)}) async-start(), calls=%async_computation.17 | async-start | bytes 2621440 | tf_op jit(solution)/shard_map/reduce_scatter | solution.py:186
  431.5 8.0 copy-start.25
  443.2 130.6 %reduce-scatter.23.cloned.1.call-start = ((), (), s32[]{:S(2)}) async-start(), calls=%async_computation.20 | async-start | bytes 4718592 | tf_op jit(solution)/shard_map/reduce_scatter | solution.py:191
  449.9 209.9 %reduce-scatter.21.cloned.1.call-start = ((), (), s32[]{:S(2)}) async-start(), calls=%async_computation.19 | async-start | bytes 4718592 | tf_op jit(solution)/shard_map/reduce_scatter | solution.py:190
  457.1 347.7 %reduce-scatter.29.cloned.1.call-start = ((), (), s32[]{:S(2)}) async-start(), calls=%async_computation.23 | async-start | bytes 4325376
  478.8 3.9 copy-start.3
  490.9 455.0 %reduce-scatter.27.cloned.1.call-start = ((), (), s32[]{:S(2)}) async-start(), calls=%async_computation.22 | async-start | bytes 4325376
  506.1 580.9 %reduce-scatter.25.cloned.1.call-start = ((), (), s32[]{:S(2)}) async-start(), calls=%async_computation.21 | async-start | bytes 4325376
  516.8 711.6 %reduce-scatter.19.cloned.1.call-start = ((), (), s32[]{:S(2)}) async-start(), calls=%async_computation.18 | async-start | bytes 4325376 | tf_op jit(solution)/shard_map/reduce_scatter | solution.py:250
  520.5 47.3 %copy-start.12 = (bf16[16,64,256]{2,1,0:T(8,128)(2,1)S(1)}, bf16[16,64,256]{2,1,0:T(8,128)(2,1)}, u32[]{:S(2)}) copy-start(bf16[16,64,256]{2,1,0:T(8,128)(2,1)} %copy-done.11) | copy-start | bytes 1572868
  (19 other events, 31.1 us)
Sparse Core Ops, SparseCore 0:
  10.9 59.1 all-gather.11
  72.9 55.1 all-gather.13
  131.0 55.0 all-gather.9
  188.8 55.0 all-gather.15
  245.9 48.0 all-gather.19
  296.0 21.1 all-gather.17
  319.2 50.3 all-gather.21
  375.6 29.3 reduce-scatter.14
  408.9 22.5 all-gather.23
  443.4 31.1 reduce-scatter.16
  478.7 89.1 reduce-scatter.22
  572.0 87.6 reduce-scatter.20
  662.6 142.1 reduce-scatter.28
  807.5 138.3 reduce-scatter.26
  948.6 138.4 reduce-scatter.24
  1089.8 138.5 reduce-scatter.18
where the time goes:
time: 1240 us; the launch traced here: 1230 us
  waiting for transfers between devices  974 us (79%)
  blocking collectives  124 us (10%)
  matrix products  73.8 us (6%)
  local copies, waits for them, and re-layouts  38.8 us (3%)
  between operations  14.5 us (1%)
    unnamed x19, waiting for transfers between devices  431 us
    reduce_scatter x1, waiting for transfers between devices, body(): lax.psum_scatter(grad_output_w, ('wide', 'ffn'), scatter_dimension=0, til...  141 us
    reduce_scatter x1, waiting for transfers between devices, body(): lax.psum_scatter(grad_up_w, 'wide', scatter_dimension=0, tiled=True)  85.9 us
    unnamed x2, blocking collectives  83.8 us
    all_gather x1, waiting for transfers between devices, body(): lax.all_gather(w_value, ('wide', 'ffn'), axis=0, tiled=True)  55.5 us
    all_gather x1, waiting for transfers between devices, body(): lax.all_gather(w_key, ('wide', 'ffn'), axis=0, tiled=True)  55.4 us
    all_gather x1, waiting for transfers between devices, body(): lax.all_gather(w_output, ('wide', 'ffn'), axis=0, tiled=True)  51.6 us
    all_gather x1, waiting for transfers between devices, body(): lax.all_gather(w_down, 'wide', axis=1, tiled=True)  45 us
  transfers between devices with their start and end apart: 16, of which 15 were waited for; matrix products, arithmetic and copies ran while one was open for 8% of the time, Pallas kernels for 0%

commit v1 on v0

--- a/solution.py
+++ b/solution.py
@@ -8,6 +8,27 @@
 HEADS = 16
 HEAD_DIM = 64
 norm_eps = 1e-12
+
+
+def gather_around(x, axis, dim):
+    size, index, extent = (lax.axis_size(axis), lax.axis_index(axis), x.shape[dim])
+    forward = [(i, (i + 1) % size) for i in range(size)]
+    left = [(i, (i - 1) % size) for i in range(size)]
+    result = jnp.zeros((*x.shape[:dim], size * extent, *x.shape[dim + 1 :]), x.dtype)
+    result = lax.dynamic_update_slice_in_dim(result, x, index * extent, axis=dim)
+    from_left = from_right = x
+    half = size // 2
+    for turn in range(1, half + 1):
+        from_left = lax.ppermute(from_left, axis, forward)
+        result = lax.dynamic_update_slice_in_dim(
+            result, from_left, (index - turn) % size * extent, axis=dim
+        )
+        if turn < size - half:
+            from_right = lax.ppermute(from_right, axis, left)
+            result = lax.dynamic_update_slice_in_dim(
+                result, from_right, (index + turn) % size * extent, axis=dim
+            )
+    return result
 
 
 def matmul(left, right):
@@ -117,7 +138,7 @@
     ) = [vector.astype(jnp.float32) for vector in gathered[4:]]
     up_part, down_part = (
         lax.all_gather(w_up, "wide", axis=0, tiled=True),
-        lax.all_gather(w_down, "wide", axis=1, tiled=True),
+        gather_around(w_down, "wide", 1),
     )
     row_count = hidden_in.shape[0]
     score_scale = HEAD_DIM ** (-0.5)

time: 1240 us -> 1210 us (0.976)
  waiting for transfers between devices: 974 us -> 920 us
  starting transfers between devices: 0.86 us -> 18 us
    all_gather x1 -> x0, waiting for transfers between devices: 45 us -> none  [body(): lax.all_gather(w_down, 'wide', axis=1, tiled=True)]
    all_gather x1, waiting for transfers between devices: 23.2 us -> 0.01 us  [body(): group_rows = lax.all_gather(normed_low, 'ffn', axis=0, tiled=True)]
    ppermute x0 -> x7, waiting for transfers between devices: none -> 22.2 us  [the longest x4 22.2 us: gather_around(): from_left = lax.ppermute(from_left, axis, forward)]
    ppermute x0 -> x7, starting transfers between devices: none -> 17.2 us  [the longest x3 10.3 us: gather_around(): from_right = lax.ppermute(from_right, axis, left)]
    unnamed x19 -> x18, waiting for transfers between devices: 431 us -> 429 us
    unnamed x82 -> x86, local copies, waits for them, and re-layouts: 37.5 us -> 37.6 us
  transfers between devices with their start and end apart: 16 -> 22, of which waited for: 15 -> 15; matrix products, arithmetic and copies ran while one was open for 8% -> 8% of each run, Pallas kernels for 0% -> 0%
where the time goes in v1:
time: 1210 us; the launch traced here: 1200 us
  waiting for transfers between devices  920 us (76%)
  blocking collectives  123 us (10%)
  matrix products  72.4 us (6%)
  local copies, waits for them, and re-layouts  46.4 us (4%)
  starting transfers between devices  18 us (1%)
  between operations  14.8 us (1%)
    unnamed x18, waiting for transfers between devices  429 us
    reduce_scatter x1, waiting for transfers between devices, body(): lax.psum_scatter(grad_output_w, ('wide', 'ffn'), scatter_dimension=0, til...  141 us
    reduce_scatter x1, waiting for transfers between devices, body(): lax.psum_scatter(grad_up_w, 'wide', scatter_dimension=0, tiled=True)  87.8 us
    unnamed x2, blocking collectives  83.4 us
    all_gather x1, waiting for transfers between devices, body(): lax.all_gather(w_value, ('wide', 'ffn'), axis=0, tiled=True)  55.5 us
    all_gather x1, waiting for transfers between devices, body(): lax.all_gather(w_key, ('wide', 'ffn'), axis=0, tiled=True)  55.4 us
    all_gather x1, waiting for transfers between devices, body(): lax.all_gather(w_output, ('wide', 'ffn'), axis=0, tiled=True)  51.6 us
    all_gather x1, blocking collectives, body(): lax.all_gather(b_up, ('wide', 'ffn'), axis=0, tiled=True)  39.6 us
  transfers between devices with their start and end apart: 22, of which 15 were waited for; matrix products, arithmetic and copies ran while one was open for 8% of the time, Pallas kernels for 0%

profile of v1, /device:TPU:0, one launch (start us, length us, event | category | flops | bytes accessed | tf_op | source)
XLA Modules:
  0.0 1204.1 jit_solution(4756584306294160066)
XLA Ops:
  17.3 42.2 %all-reduce.18 = (bf16[1024]{0:T(1024)(128)(2,1)S(1)}, bf16[1024]{0:T(1024)(128)(2,1)S(1)}, bf16[1024]{0:T(1024)(128)(2,1)S(1)}, bf16[1024]{0:T(1024)(128)(2,1)S...) all-reduce(bf16[1024]{0:T(1024)(128)(2,1)S(1)} %dynamic-update-slic, ...), channel_id=1, replica_groups=mesh['wide'=8,'ffn'=4] {'wide','ffn'}, use_global_device_ids=true, to_apply=%add | all-reduce | flops 8192 | bytes 32768
  60.5 9.6 all-gather.11.cloned.1.call-done
  72.7 55.4 %all-gather.13.cloned.1.call-done = bf16[1024,1024]{1,0:T(8,128)(2,1)} async-done(((bf16[32,1024]{1,0:T(8,128)(2,1)}), bf16[1024,1024]{1,0:T(8,128)(2,1)}) %all-gather.13.cloned.1.call-update) | async-done | bytes 2097168 | tf_op jit(solution)/shard_map/all_gather | solution.py:109
  130.6 55.5 %all-gather.9.cloned.1.call-done = bf16[1024,1024]{1,0:T(8,128)(2,1)} async-done(((bf16[32,1024]{1,0:T(8,128)(2,1)}), bf16[1024,1024]{1,0:T(8,128)(2,1)}) %all-gather.9.cloned.1.call-update) | async-done | bytes 2097168 | tf_op jit(solution)/shard_map/all_gather | solution.py:110
  192.3 51.6 %all-gather.15.cloned.1.call-done = bf16[1024,1024]{1,0:T(8,128)(2,1)} async-done(((bf16[32,1024]{1,0:T(8,128)(2,1)}), bf16[1024,1024]{1,0:T(8,128)(2,1)}) %all-gather.15.cloned.1.call-update) | async-done | bytes 2097168 | tf_op jit(solution)/shard_map/all_gather | solution.py:111
  252.6 11.1 collective-permute-done
  270.7 39.6 %all-gather = bf16[32,1,128]{2,1,0:T(2,128)(2,1)S(1)} all-gather(bf16[1,1,128]{2,1,0:T(2,128)(2,1)S(1)} %bitcast.90), channel_id=1, replica_groups=mesh['wide'=8,'ffn'=4] {'wide','ffn'}, dimensions={0}, use_global_device_ids=true | all-gather | bytes 8448 | tf_op jit(solution)/shard_map/all_gather | solution.py:117
  327.7 6.2 collective-permute-done.6
  334.6 6.8 multiply_convert_fusion.1
  348.1 27.1 %reduce-scatter.15.cloned.1.call-done = bf16[256,1024]{1,0:T(8,128)(2,1)} async-done(((bf16[1024,1024]{1,0:T(8,128)(2,1)}), bf16[256,1024]{1,0:T(8,128)(2,1)}) %reduce-scatter.15.cloned.1.call-update) | async-done | bytes 524304 | tf_op jit(solution)/shard_map/reduce_scatter | solution.py:184
  379.0 22.6 %all-gather.21.cloned.1.call-done = bf16[1024,1024]{1,0:T(8,128)(2,1)} async-done(((bf16[256,1024]{1,0:T(8,128)(2,1)}), bf16[1024,1024]{1,0:T(8,128)(2,1)}) %all-gather.21.cloned.1.call-update) | async-done | bytes 2097168 | tf_op jit(solution)/shard_map/all_gather | solution.py:199
  401.7 6.6 convert_reduce_fusion
  413.4 6.6 fusion.38
  420.2 7.0 fusion.37
  427.3 17.4 %reduce-scatter.17.cloned.1.call-done = bf16[256,1024]{1,0:T(8,128)(2,1)} async-done(((bf16[1024,1024]{1,0:T(8,128)(2,1)}), bf16[256,1024]{1,0:T(8,128)(2,1)}) %reduce-scatter.17.cloned.1.call-update) | async-done | bytes 524304 | tf_op jit(solution)/shard_map/reduce_scatter | solution.py:207
  455.0 5.7 copy.80
  470.0 5.4 copy.78
  479.8 5.4 copy.76
  489.8 41.1 %all-reduce.17 = (f32[1024]{0:T(1024)S(1)}, f32[1024]{0:T(1024)S(1)}, f32[1024]{0:T(1024)S(1)}, f32[1024]{0:T(1024)S(1)}, f32[1024]{0:T(1024)S(1)}, /*index=5*/f...) all-reduce(f32[1024]{0:T(1024)S(1)} %reduce_sum.186, ...), channel_id=5, replica_groups=mesh['wide'=8,'ffn'=4] {'wide','ffn'}, use_global_device_ids=true, to_apply=%region_15.16.clone | all-reduce | flops 12288 | bytes 98304
  542.2 87.8 %reduce-scatter.21.cloned.1.call-done = f32[128,1024]{1,0:T(8,128)} async-done(((f32[1024,1024]{1,0:T(8,128)}), f32[128,1024]{1,0:T(8,128)}) %reduce-scatter.21.cloned.1.call-update) | async-done | bytes 524304 | tf_op jit(solution)/shard_map/reduce_scatter | solution.py:211
  630.1 144.2 %reduce-scatter.29.cloned.1.call-done = f32[32,1024]{1,0:T(8,128)} async-done(((f32[1024,1024]{1,0:T(8,128)}), f32[32,1024]{1,0:T(8,128)}) %reduce-scatter.29.cloned.1.call-update) | async-done | bytes 131088
  774.3 141.2 %reduce-scatter.27.cloned.1.call-done = f32[32,1024]{1,0:T(8,128)} async-done(((f32[1024,1024]{1,0:T(8,128)}), f32[32,1024]{1,0:T(8,128)}) %reduce-scatter.27.cloned.1.call-update) | async-done | bytes 131088
  915.5 140.8 %reduce-scatter.25.cloned.1.call-done = f32[32,1024]{1,0:T(8,128)} async-done(((f32[1024,1024]{1,0:T(8,128)}), f32[32,1024]{1,0:T(8,128)}) %reduce-scatter.25.cloned.1.call-update) | async-done | bytes 131088
  1056.3 141.1 %reduce-scatter.19.cloned.1.call-done = f32[32,1024]{1,0:T(8,128)} async-done(((f32[1024,1024]{1,0:T(8,128)}), f32[32,1024]{1,0:T(8,128)}) %reduce-scatter.19.cloned.1.call-update) | async-done | bytes 131088 | tf_op jit(solution)/shard_map/reduce_scatter | solution.py:271
  (194 shorter events, 111.3 us)
Async XLA Ops:
  7.2 62.8 %all-gather.11.cloned.1.call-start = ((), (), s32[]{:S(2)}) async-start(), calls=%async_computation.9 | async-start | bytes 2162688 | tf_op jit(solution)/shard_map/all_gather | solution.py:108
  7.9 120.2 %all-gather.13.cloned.1.call-start = ((), (), s32[]{:S(2)}) async-start(), calls=%async_computation.10 | async-start | bytes 2162688 | tf_op jit(solution)/shard_map/all_gather | solution.py:109
  8.7 177.4 %all-gather.9.cloned.1.call-start = ((), (), s32[]{:S(2)}) async-start(), calls=%async_computation.8 | async-start | bytes 2162688 | tf_op jit(solution)/shard_map/all_gather | solution.py:110
  9.4 234.5 %all-gather.15.cloned.1.call-start = ((), (), s32[]{:S(2)}) async-start(), calls=%async_computation.11 | async-start | bytes 2162688 | tf_op jit(solution)/shard_map/all_gather | solution.py:111
  10.0 324.6 %all-gather.19.cloned.1.call-start = ((), (), s32[]{:S(2)}) async-start(), calls=%async_computation.13 | async-start | bytes 2359296 | tf_op jit(solution)/shard_map/all_gather | solution.py:140
  10.6 324.0 %all-gather.17.cloned.1.call-start = ((), (), s32[]{:S(2)}) async-start(), calls=%async_computation.12 | async-start | bytes 2621440 | tf_op jit(solution)/shard_map/all_gather | solution.py:180
  60.4 67.7 %copy-start.4 = (bf16[256,1024]{1,0:T(8,128)(2,1)S(1)}, bf16[256,1024]{1,0:T(8,128)(2,1)}, u32[]{:S(2)}) copy-start(bf16[256,1024]{1,0:T(8,128)(2,1)} %param.18) | copy-start | bytes 1572868
  72.7 115.9 %copy-start.14 = (bf16[256,1024]{0,1:T(8,128)(2,1)}, bf16[256,1024]{0,1:T(8,128)(2,1)S(1)}, u32[]{:S(2)}) copy-start(bf16[256,1024]{0,1:T(8,128)(2,1)S(1)} %copy.62) | copy-start | bytes 1572868
  247.7 127.4 %reduce-scatter.15.cloned.1.call-start = ((), (), s32[]{:S(2)}) async-start(), calls=%async_computation.14 | async-start | bytes 2621440 | tf_op jit(solution)/shard_map/reduce_scatter | solution.py:184
  247.8 15.9 %collective-permute-start = (bf16[1024,128]{1,0:T(8,128)(2,1)S(1)}, bf16[1024,128]{1,0:T(8,128)(2,1)S(1)}, u32[]{:S(2)}, u32[]{:S(2)}) collective-permute-start(bf16[1024,128]{1,0:T(8,128)(2,1)S(1)} %copy-done.24), channel_id=1, source_target_pairs={{0,4},{4,8},{8,12},{12,16},{16,20},{20,24},{24,28},{28,0},{1,5},{5... | collective-permute-start | bytes 786440 | tf_op jit(solution)/shard_map/ppermute | solution.py:22
  249.3 16.9 %collective-permute-start.1 = (bf16[1024,128]{1,0:T(8,128)(2,1)S(1)}, bf16[1024,128]{1,0:T(8,128)(2,1)S(1)}, u32[]{:S(2)}, u32[]{:S(2)}) collective-permute-start(bf16[1024,128]{1,0:T(8,128)(2,1)S(1)} %copy-done.24), channel_id=1, source_target_pairs={{0,28},{4,0},{8,4},{12,8},{16,12},{20,16},{24,20},{28,24},{1,29},{... | collective-permute-start | bytes 786440 | tf_op jit(solution)/shard_map/ppermute | solution.py:27
  263.7 46.8 %collective-permute-start.2 = (bf16[1024,128]{1,0:T(8,128)(2,1)S(1)}, bf16[1024,128]{1,0:T(8,128)(2,1)S(1)}, u32[]{:S(2)}, u32[]{:S(2)}) collective-permute-start(bf16[1024,128]{1,0:T(8,128)(2,1)S(1)} %collective-permute-done), channel_id=1, source_target_pairs={{0,4},{4,8},{8,12},{12,16},{16,20},{20,24},{24,28},{28,0},{1,5},{5... | collective-permute-start | bytes 786440 | tf_op jit(solution)/shard_map/ppermute | solution.py:22
  266.1 45.8 %collective-permute-start.3 = (bf16[1024,128]{1,0:T(8,128)(2,1)S(1)}, bf16[1024,128]{1,0:T(8,128)(2,1)S(1)}, u32[]{:S(2)}, u32[]{:S(2)}) collective-permute-start(bf16[1024,128]{1,0:T(8,128)(2,1)S(1)} %collective-permute-done.1), channel_id=1, source_target_pairs={{0,28},{4,0},{8,4},{12,8},{16,12},{20,16},{24,20},{28,24},{1,29},{... | collective-permute-start | bytes 786440 | tf_op jit(solution)/shard_map/ppermute | solution.py:27
  310.5 12.0 collective-permute-start.4
  312.0 14.9 %collective-permute-start.5 = (bf16[1024,128]{1,0:T(8,128)(2,1)S(1)}, bf16[1024,128]{1,0:T(8,128)(2,1)S(1)}, u32[]{:S(2)}, u32[]{:S(2)}) collective-permute-start(bf16[1024,128]{1,0:T(8,128)(2,1)S(1)} %collective-permute-done.3), channel_id=1, source_target_pairs={{0,28},{4,0},{8,4},{12,8},{16,12},{20,16},{24,20},{28,24},{1,29},{... | collective-permute-start | bytes 786440 | tf_op jit(solution)/shard_map/ppermute | solution.py:27
  322.5 11.4 collective-permute-start.6
  348.0 53.7 %all-gather.21.cloned.1.call-start = ((), (), s32[]{:S(2)}) async-start(), calls=%async_computation.15 | async-start | bytes 2621440 | tf_op jit(solution)/shard_map/all_gather | solution.py:199
  379.0 65.7 %reduce-scatter.17.cloned.1.call-start = ((), (), s32[]{:S(2)}) async-start(), calls=%async_computation.16 | async-start | bytes 2621440 | tf_op jit(solution)/shard_map/reduce_scatter | solution.py:207
  413.4 128.9 %reduce-scatter.23.cloned.1.call-start = ((), (), s32[]{:S(2)}) async-start(), calls=%async_computation.19 | async-start | bytes 4718592 | tf_op jit(solution)/shard_map/reduce_scatter | solution.py:212
  420.0 210.1 %reduce-scatter.21.cloned.1.call-start = ((), (), s32[]{:S(2)}) async-start(), calls=%async_computation.18 | async-start | bytes 4718592 | tf_op jit(solution)/shard_map/reduce_scatter | solution.py:211
  427.2 347.1 %reduce-scatter.29.cloned.1.call-start = ((), (), s32[]{:S(2)}) async-start(), calls=%async_computation.22 | async-start | bytes 4325376
  460.7 454.8 %reduce-scatter.27.cloned.1.call-start = ((), (), s32[]{:S(2)}) async-start(), calls=%async_computation.21 | async-start | bytes 4325376
  475.4 580.9 %reduce-scatter.25.cloned.1.call-start = ((), (), s32[]{:S(2)}) async-start(), calls=%async_computation.20 | async-start | bytes 4325376
  485.3 712.1 %reduce-scatter.19.cloned.1.call-start = ((), (), s32[]{:S(2)}) async-start(), calls=%async_computation.17 | async-start | bytes 4325376 | tf_op jit(solution)/shard_map/reduce_scatter | solution.py:271
  (27 other events, 257.5 us)
Sparse Core Ops, SparseCore 0:
  10.9 59.1 all-gather.10
  72.9 55.1 all-gather.12
  131.0 55.0 all-gather.8
  188.8 55.0 all-gather.14
  245.9 55.9 all-gather.18
  303.9 21.0 all-gather.16
  348.1 27.0 reduce-scatter.14
  379.1 22.5 all-gather.20
  413.5 31.1 reduce-scatter.16
  448.7 89.0 reduce-scatter.22
  542.1 87.9 reduce-scatter.20
  632.8 141.4 reduce-scatter.28
  777.2 138.2 reduce-scatter.26
  918.2 138.0 reduce-scatter.24
  1059.0 138.3 reduce-scatter.18
